TPU v7x, 256 devices: a whole 4x4x8 slice. The times are simulated.
256 devices in a mesh: group: 32 (over x, y, core), tp: 8 (over z).
Axes of the slice: x: 4, y: 4, z: 8, core: 2. Of those that a mesh axis runs over, the one named last changes fastest.
Arguments:
- hidden_in: bfloat16 [64, 3072], P('group'), may hold values from -6 to 6
- w_qkv: bfloat16 [3072, 2048], P(None, 'tp'), may hold values from -0.109375 to 0.109375
- w_out: bfloat16 [1536, 3072], P('tp'), may hold values from -0.15625 to 0.15625
- kv_pool: bfloat16 [2048, 128, 512], P(('group', 'tp'))
- page_table: int32 [64, 32], replicated, may hold values from 0 to 2047, as said below
- lengths: int32 [64], replicated, may hold values from 1 to 4096, as said below
Outputs:
- attn_proj: bfloat16 [64, 3072], P('group', 'tp')
Inputs may be any that keep to these rules, and one draw needn't show every extreme that they name: `page_table`: every pool slot is named by exactly one request page. `lengths`: some request has the full 32 * 128 cached tokens.
All inputs are finite; a program needn't handle non-finite values.
Results may differ from a plain program's by a relative error of at most 0.0085.
The roundings to bfloat16 on the way count: a program that leaves them out, or rounds other values in their place, can miss the bound.
Values may be sent and summed in bfloat16 or wider, within the bound.
A program may use at most 64 MiB of HBM per device.

v0:
```python
import jax
import jax.numpy as jnp
from jax import lax
from jax.sharding import PartitionSpec as P

HEADS = 12
KV_HEADS = 2
HEAD_DIM = 128


def on_device(hidden_in, w_qkv, w_out, kv_pool, page_table, lengths):
    qdim = HEADS * HEAD_DIM
    kdim = KV_HEADS * HEAD_DIM
    per_kv = HEADS // KV_HEADS
    scale = HEAD_DIM ** (-0.5)
    req_grp = hidden_in.shape[0]
    col_count = w_out.shape[0]
    col_start = lax.axis_index("tp") * col_count
    columns = jnp.dot(hidden_in, w_qkv, preferred_element_type=jnp.float32).astype(jnp.bfloat16)
    qkv = lax.all_gather(columns, "tp", axis=1, tiled=True)
    queries = lax.all_gather(qkv[:, :qdim], "group", axis=0, tiled=True)
    requests = queries.shape[0]
    slot_count = kv_pool.shape[0]
    page_len = kv_pool.shape[1]
    max_pages = page_table.shape[1]
    slot_ids = lax.axis_index(("group", "tp")) * slot_count + jnp.arange(
        slot_count, dtype=jnp.int32
    )
    match = page_table[:, :, None] == slot_ids[None, None, :]
    slot_req = jnp.sum(
        jnp.where(match, jnp.arange(requests, dtype=jnp.int32)[:, None, None], 0), axis=(0, 1)
    )
    slot_page = jnp.sum(
        jnp.where(match, jnp.arange(max_pages, dtype=jnp.int32)[None, :, None], 0), axis=(0, 1)
    )
    chosen = queries[slot_req].reshape(slot_count, KV_HEADS, per_kv, HEAD_DIM)
    keys = kv_pool[..., :kdim].reshape(slot_count, page_len, KV_HEADS, HEAD_DIM)
    values = kv_pool[..., kdim:].reshape(slot_count, page_len, KV_HEADS, HEAD_DIM)
    scores = jnp.einsum("pgjd,ptgd->pgjt", chosen, keys, preferred_element_type=jnp.float32) * scale
    position = slot_page[:, None] * page_len + jnp.arange(page_len, dtype=jnp.int32)[None, :]
    live = (position < lengths[slot_req][:, None])[:, None, None, :]
    top = jnp.max(jnp.where(live, scores, -1e30), axis=-1)
    probs = jnp.where(live, jnp.exp(scores - top[..., None]), 0.0).astype(jnp.bfloat16)
    total = jnp.sum(probs.astype(jnp.float32), axis=-1)
    weighted = jnp.einsum("pgjt,ptgd->pgjd", probs, values, preferred_element_type=jnp.float32)
    owner = slot_req[None, :] == jnp.arange(requests, dtype=jnp.int32)[:, None]
    req_top = jnp.max(jnp.where(owner[:, :, None, None], top[None], -1e30), axis=1)
    factor = jnp.exp(top - req_top[slot_req])
    onehot = owner.astype(jnp.float32)
    req_total = jnp.einsum(
        "rp,pgj->rgj", onehot, total * factor, precision=lax.Precision.HIGHEST
    ).reshape(requests, HEADS)
    req_sums = jnp.einsum(
        "rp,pgjd->rgjd", onehot, weighted * factor[..., None], precision=lax.Precision.HIGHEST
    ).reshape(requests, qdim)
    req_top = req_top.reshape(requests, HEADS)
    start = lax.axis_index("group") * req_grp
    peak_all = lax.pmax(req_top, ("group", "tp"))
    rescale = jnp.exp(req_top - peak_all)
    total_all, sums_all = lax.psum(
        (req_total * rescale, req_sums * jnp.repeat(rescale, HEAD_DIM, axis=1)), ("group", "tp")
    )
    peak = lax.dynamic_slice_in_dim(peak_all, start, req_grp, 0)
    whole = lax.dynamic_slice_in_dim(total_all, start, req_grp, 0)
    sums = lax.dynamic_slice_in_dim(sums_all, start, req_grp, 0)
    sums_part = lax.dynamic_slice_in_dim(sums, col_start, col_count, 1)
    own_q = qkv[:, :qdim].reshape(req_grp, KV_HEADS, per_kv, HEAD_DIM)
    own_k = qkv[:, qdim : qdim + kdim].reshape(req_grp, KV_HEADS, HEAD_DIM)
    own_v = qkv[:, qdim + kdim :].reshape(req_grp, KV_HEADS, HEAD_DIM)
    own_score = (
        jnp.einsum("rgjd,rgd->rgj", own_q, own_k, preferred_element_type=jnp.float32) * scale
    ).reshape(req_grp, HEADS)
    own_sums = jnp.broadcast_to(
        own_v.astype(jnp.float32)[:, :, None, :], (req_grp, KV_HEADS, per_kv, HEAD_DIM)
    ).reshape(req_grp, qdim)
    new_peak = jnp.maximum(peak, own_score)
    old_factor = jnp.exp(peak - new_peak)
    own_factor = jnp.exp(own_score - new_peak)
    new_whole = whole * old_factor + own_factor

    def pick(values_full):
        return lax.dynamic_slice_in_dim(values_full, col_start, col_count, 1)

    new_sums = sums_part * pick(jnp.repeat(old_factor, HEAD_DIM, axis=1)) + pick(
        own_sums * jnp.repeat(own_factor, HEAD_DIM, axis=1)
    )
    attn_part = (new_sums / pick(jnp.repeat(new_whole, HEAD_DIM, axis=1))).astype(jnp.bfloat16)
    partial_value = jnp.dot(attn_part, w_out, preferred_element_type=jnp.float32)
    return lax.psum_scatter(partial_value, "tp", scatter_dimension=1, tiled=True).astype(
        jnp.bfloat16
    )


def solution(mesh):
    in_specs = (
        P("group", None),
        P(None, "tp"),
        P("tp", None),
        P(("group", "tp"), None, None),
        P(),
        P(),
    )
    out_specs = P("group", "tp")
    return jax.shard_map(
        on_device, mesh=mesh, in_specs=in_specs, out_specs=out_specs, check_vma=False
    )
```

profile of v0, /device:TPU:2, one launch (start us, length us, event | category | flops | bytes accessed | tf_op | source)
XLA Modules:
  0.0 429.0 jit_solution(9588263399593622062)
XLA Ops:
  6.5 1.1 fusion.1
  7.7 0.2 copy-done
  8.0 1.0 convolution_convert_fusion
  9.0 19.1 %all_gather.6 = bf16[2,2048]{1,0:T(2,128)(2,1)S(1)} all-gather(bf16[2,256]{1,0:T(2,128)(2,1)S(1)} %convolution_convert_fusion), channel_id=1, replica_groups=mesh['group'=32,'tp'=8] {'tp'}, dimensions={1}, use_global_device_ids=true | all-gather | bytes 9216 | tf_op jit(solution)/shard_map/all_gather | solution.py:20
  28.1 24.7 %all-gather = bf16[32,2,1536]{2,1,0:T(2,128)(2,1)S(1)} all-gather(bf16[1,2,1536]{2,1,0:T(2,128)(2,1)S(1)} %get-tuple-element.19), channel_id=1, replica_groups=mesh['group'=32,'tp'=8] {'group'}, dimensions={0}, use_global_device_ids=true | all-gather | bytes 202752 | tf_op jit(solution)/shard_map/all_gather | solution.py:21
  52.9 0.6 gather_fusion
  53.5 0.6 gather_fusion.1
  54.1 1.3 fusion.25
  55.4 0.3 copy.96
  55.8 0.3 select_reduce_fusion
  56.4 0.3 copy.97
  56.7 0.2 convert_reduce_fusion
  57.0 74.0 %pmax.7 = f32[64,12]{1,0:T(8,128)S(1)} all-reduce(f32[64,12]{1,0:T(8,128)S(1)} %copy.86), channel_id=1, replica_groups=mesh['group'=32,'tp'=8] {'group','tp'}, use_global_device_ids=true, to_apply=%region_4.5 | all-reduce | flops 768 | bytes 6144 | tf_op jit(solution)/shard_map/pmax | solution.py:58
  131.0 0.6 gather_fusion.2
  131.9 0.4 convolution_multiply_fusion
  132.3 0.4 fusion.2
  132.8 0.2 copy.84
  133.2 0.2 broadcast_in_dim.104
  133.4 0.9 bitcast_multiply_fusion
  134.6 74.9 %psum.15 = f32[64,12]{1,0:T(8,128)S(1)} all-reduce(f32[64,12]{1,0:T(8,128)S(1)} %get-tuple-element.10), channel_id=1, replica_groups=mesh['group'=32,'tp'=8] {'group','tp'}, use_global_device_ids=true, to_apply=%region_7.8 | all-reduce | flops 768 | bytes 6144 | tf_op jit(solution)/shard_map/psum | solution.py:60
  209.7 168.6 %all-reduce.2.cloned.1.call-done = f32[64,1536]{1,0:T(8,128)} async-done(((f32[64,1536]{1,0:T(8,128)}), f32[64,1536]{1,0:T(8,128)}) %all-reduce.2.cloned.1.call-update) | async-done | bytes 393232 | tf_op jit(solution)/shard_map/psum | solution.py:60
  378.3 2.7 convolution_bitcast_fusion
  381.0 39.5 %reduce-scatter.4.cloned.1.call-done = f32[384,2]{1,0:T(8,128)} async-done(((f32[3072,2]{1,0:T(8,128)}), f32[384,2]{1,0:T(8,128)}) %reduce-scatter.4.cloned.1.call-update) | async-done | bytes 3088
  420.5 1.6 copy.95
  (43 shorter events, 1.6 us)
Async XLA Ops:
  6.5 1.4 copy-start
  6.5 46.4 %copy-start.1 = (s32[64]{0:T(128)S(1)}, s32[64]{0:T(128)}, u32[]{:S(2)}) copy-start(s32[64]{0:T(128)} %param.11) | copy-start | bytes 772
  6.5 371.7 %all-reduce.2.cloned.1.call-start = ((), (), s32[]{:S(2)}) async-start(), calls=%async_computation.1 | async-start | bytes 786432 | tf_op jit(solution)/shard_map/psum | solution.py:60
  133.1 245.2 %copy-start.2 = (bf16[192,3072]{1,0:T(8,128)(2,1)S(1)}, bf16[192,3072]{1,0:T(8,128)(2,1)}, u32[]{:S(2)}) copy-start(bf16[192,3072]{1,0:T(8,128)(2,1)} %param.8) | copy-start | bytes 3538948
  134.3 286.2 %reduce-scatter.4.cloned.1.call-start = ((), (), s32[]{:S(2)}) async-start(), calls=%async_computation.2 | async-start | bytes 1769472
Sparse Core Ops, SparseCore 0:
  134.4 243.8 all-reduce.1
  381.1 39.3 reduce-scatter.3
where the time goes:
time: 430 us; the launch traced here: 429 us
  waiting for transfers between devices  208 us (48%)
  blocking collectives  193 us (45%)
  between operations  13.6 us (3%)
  local copies, waits for them, and re-layouts  6.81 us (2%)
  matrix products  5.21 us (1%)
    psum x1, waiting for transfers between devices, on_device(): lax.psum((req_total * rescale, req_sums * jnp.repeat(rescale, HEAD_DIM, a...  169 us
    psum x1, blocking collectives, on_device(): lax.psum((req_total * rescale, req_sums * jnp.repeat(rescale, HEAD_DIM, a...  74.9 us
    pmax x1, blocking collectives, on_device(): peak_all = lax.pmax(req_top, ('group', 'tp'))  74 us
    unnamed x3, waiting for transfers between devices  39.6 us
    all_gather x1, blocking collectives, on_device(): queries = lax.all_gather(qkv[:, :qdim], 'group', axis=0, tiled=True)  24.7 us
    all_gather x1, blocking collectives, on_device(): qkv = lax.all_gather(columns, 'tp', axis=1, tiled=True)  19.1 us
  transfers between devices with their start and end apart: 2, of which 2 were waited for; matrix products, arithmetic and copies ran while one was open for 0% of the time, Pallas kernels for 0%

commit v1 on v0

--- a/solution.py
+++ b/solution.py
@@ -18,7 +18,13 @@
     col_start = lax.axis_index("tp") * col_count
     columns = jnp.dot(hidden_in, w_qkv, preferred_element_type=jnp.float32).astype(jnp.bfloat16)
     qkv = lax.all_gather(columns, "tp", axis=1, tiled=True)
-    queries = lax.all_gather(qkv[:, :qdim], "group", axis=0, tiled=True)
+    payload = qkv[:, :qdim]
+    queries = jnp.concatenate(
+        lax.all_to_all(
+            jnp.stack(tuple((payload for _ in range(lax.axis_size("group"))))), "group", 0, 0
+        ),
+        axis=0,
+    )
     requests = queries.shape[0]
     slot_count = kv_pool.shape[0]
     page_len = kv_pool.shape[1]

time: 430 us -> 491 us (1.14)
  waiting for transfers between devices: 208 us -> 287 us
  blocking collectives: 193 us -> 167 us
  starting transfers between devices: 0.04 us -> 7.71 us
    psum x1, waiting for transfers between devices: 169 us -> 243 us  [on_device(): lax.psum((req_total * rescale, req_sums * jnp.repeat(rescale, HEAD_DIM, a...]
    all_gather x1 -> x0, blocking collectives: 24.7 us -> none  [on_device(): queries = lax.all_gather(qkv[:, :qdim], 'group', axis=0, tiled=True)]
    all_to_all x0 -> x1, starting transfers between devices: none -> 7.62 us  [on_device(): lax.all_to_all(jnp.stack(tuple((payload for _ in range(lax.axis_size('gro...]
  transfers between devices with their start and end apart: 2 -> 3, of which waited for: 2 -> 3; matrix products, arithmetic and copies ran while one was open for 0% -> 1% of each run, Pallas kernels for 0% -> 0%
where the time goes in v1:
time: 491 us; the launch traced here: 490 us
  waiting for transfers between devices  287 us (58%)
  blocking collectives  167 us (34%)
  between operations  13.6 us (3%)
  local copies, waits for them, and re-layouts  8.81 us (2%)
  starting transfers between devices  7.71 us (2%)
  matrix products  5.19 us (1%)
    psum x1, waiting for transfers between devices, on_device(): lax.psum((req_total * rescale, req_sums * jnp.repeat(rescale, HEAD_DIM, a...  243 us
    psum x1, blocking collectives, on_device(): lax.psum((req_total * rescale, req_sums * jnp.repeat(rescale, HEAD_DIM, a...  74.5 us
    pmax x1, blocking collectives, on_device(): peak_all = lax.pmax(req_top, ('group', 'tp'))  73.4 us
    unnamed x3, waiting for transfers between devices  39.6 us
    all_gather x1, blocking collectives, on_device(): qkv = lax.all_gather(columns, 'tp', axis=1, tiled=True)  19.1 us
  transfers between devices with their start and end apart: 3, of which 3 were waited for; matrix products, arithmetic and copies ran while one was open for 1% of the time, Pallas kernels for 0%

profile of v1, /device:TPU:2, one launch (start us, length us, event | category | flops | bytes accessed | tf_op | source)
XLA Modules:
  0.0 490.4 jit_solution(3824054482936572742)
XLA Ops:
  6.5 1.4 copy-done
  7.9 1.0 convolution_convert_fusion
  9.0 19.1 %all_gather.3 = bf16[2,2048]{1,0:T(2,128)(2,1)S(1)} all-gather(bf16[2,256]{1,0:T(2,128)(2,1)S(1)} %convolution_convert_fusion), channel_id=1, replica_groups=mesh['group'=32,'tp'=8] {'tp'}, dimensions={1}, use_global_device_ids=true | all-gather | bytes 9216 | tf_op jit(solution)/shard_map/all_gather | solution.py:20
  28.1 0.8 stack.2
  28.9 7.6 %all-to-all-start = ((bf16[32,2,1536]{2,1,0:T(2,128)(2,1)}), bf16[32,2,1536]{2,1,0:T(2,128)(2,1)S(1)}, u32[]{:S(2)}, u32[]{:S(2)}) async-start(bf16[32,2,1536]{2,1,0:T(2,128)(2,1)} %stack.2), calls=%async_computation | async-start | bytes 393216 | tf_op jit(solution)/shard_map/all_to_all | solution.py:23
  36.6 0.2 fusion.1
  37.1 1.3 fusion.25
  38.4 0.3 copy.97
  38.7 0.3 copy.96
  39.1 0.6 gather_fusion
  39.9 3.8 all-to-all-done
  43.7 0.6 gather_fusion.1
  44.3 0.3 select_reduce_fusion
  45.2 73.4 %pmax.7 = f32[64,12]{1,0:T(8,128)S(1)} all-reduce(f32[64,12]{1,0:T(8,128)S(1)} %copy.86), channel_id=1, replica_groups=mesh['group'=32,'tp'=8] {'group','tp'}, use_global_device_ids=true, to_apply=%region_4.5 | all-reduce | flops 768 | bytes 6144 | tf_op jit(solution)/shard_map/pmax | solution.py:64
  118.6 0.6 gather_fusion.2
  119.5 74.5 %psum.15 = f32[64,12]{1,0:T(8,128)S(1)} all-reduce(f32[64,12]{1,0:T(8,128)S(1)} %get-tuple-element.10), channel_id=1, replica_groups=mesh['group'=32,'tp'=8] {'group','tp'}, use_global_device_ids=true, to_apply=%region_7.8 | all-reduce | flops 768 | bytes 6144 | tf_op jit(solution)/shard_map/psum | solution.py:66
  194.1 0.4 convolution_multiply_fusion
  194.5 0.4 fusion.2
  194.9 0.2 copy.84
  195.5 0.9 bitcast_multiply_fusion
  196.6 243.2 %all-reduce.2.cloned.1.call-done = f32[64,1536]{1,0:T(8,128)} async-done(((f32[64,1536]{1,0:T(8,128)}), f32[64,1536]{1,0:T(8,128)}) %all-reduce.2.cloned.1.call-update) | async-done | bytes 393232 | tf_op jit(solution)/shard_map/psum | solution.py:66
  439.8 2.7 convolution_bitcast_fusion
  442.5 39.5 %reduce-scatter.4.cloned.1.call-done = f32[384,2]{1,0:T(8,128)} async-done(((f32[3072,2]{1,0:T(8,128)}), f32[384,2]{1,0:T(8,128)}) %reduce-scatter.4.cloned.1.call-update) | async-done | bytes 3088
  482.0 1.6 copy.95
  (47 shorter events, 2.1 us)
Async XLA Ops:
  6.5 1.4 copy-start
  6.5 30.1 %copy-start.3 = (s32[64,32]{0,1:T(8,128)S(1)}, s32[64,32]{0,1:T(8,128)}, u32[]{:S(2)}) copy-start(s32[64,32]{0,1:T(8,128)} %param.10) | copy-start | bytes 24580
  28.9 14.8 %all-to-all-start = ((bf16[32,2,1536]{2,1,0:T(2,128)(2,1)}), bf16[32,2,1536]{2,1,0:T(2,128)(2,1)S(1)}, u32[]{:S(2)}, u32[]{:S(2)}) async-start(bf16[32,2,1536]{2,1,0:T(2,128)(2,1)} %stack.2), calls=%async_computation | async-start | bytes 393216 | tf_op jit(solution)/shard_map/all_to_all | solution.py:23
  36.5 403.2 %all-reduce.2.cloned.1.call-start = ((), (), s32[]{:S(2)}) async-start(), calls=%async_computation.2 | async-start | bytes 786432 | tf_op jit(solution)/shard_map/psum | solution.py:66
  38.4 0.7 copy-start.1
  195.3 244.5 %copy-start.2 = (bf16[192,3072]{1,0:T(8,128)(2,1)S(1)}, bf16[192,3072]{1,0:T(8,128)(2,1)}, u32[]{:S(2)}) copy-start(bf16[192,3072]{1,0:T(8,128)(2,1)} %param.8) | copy-start | bytes 3538948
  196.4 285.6 %reduce-scatter.4.cloned.1.call-start = ((), (), s32[]{:S(2)}) async-start(), calls=%async_computation.3 | async-start | bytes 1769472
Sparse Core Ops, SparseCore 0:
  196.6 243.1 all-reduce.1
  442.6 39.3 reduce-scatter.3
